TPU v7x, 32 devices: a whole 2x2x4 slice. The times are simulated.
32 devices in a mesh: uly: 8 (over z, y), blk: 4 (over x, core).
Axes of the slice: x: 2, y: 2, z: 4, core: 2. Of those that a mesh axis runs over, the one named last changes fastest.
Arguments:
- queries: bfloat16 [4096, 4096], P(('blk', 'uly')), may hold values from -8 to 8
- keys: bfloat16 [4096, 1024], P(('blk', 'uly')), may hold values from -8 to 8
- values: bfloat16 [4096, 1024], P(('blk', 'uly')), may hold values from -6 to 6
- live_blocks: int32 [32, 8], replicated, may hold values from 0 to 31, as said below
Outputs:
- attended: bfloat16 [4096, 4096], P(('blk', 'uly'))
Inputs may be any that keep to these rules, and one draw needn't show every extreme that they name: `live_blocks`: each row holds 8 different block numbers, among them the row's own block, the blocks just before and after it where they exist, and block 0; the others are drawn from the seed.
All inputs are finite; a program needn't handle non-finite values.
Results may differ from a plain program's by a relative error of at most 0.0049.
Values may be sent and summed in bfloat16 or wider, within the bound.
A program may use at most 128 MiB of HBM per device.

v0:
```python
from functools import partial
import math

import jax
import jax.numpy as jnp
from jax import lax
from jax.sharding import PartitionSpec as P

H = 32
KVH = 8
HD = 128
BLOCK = 128


def attend_piece(state, pieces, start, query_blocks, rows_live, score_scale):
    row_max, row_sum, accumulated = state
    key_part, value_part = pieces
    key_count = key_part.shape[0]
    block_len = query_blocks.shape[1]
    offsets = (
        rows_live[:, :, None] * block_len
        + jnp.arange(block_len, dtype=jnp.int32)[None, None, :]
        - start
    )
    inside = (offsets >= 0) & (offsets < key_count)
    picked = jnp.clip(offsets, 0, key_count - 1)
    key_rows = key_part[picked]
    value_rows = value_part[picked]
    scores = (
        jnp.einsum("qbhd,qlkhd->qhblk", query_blocks, key_rows, preferred_element_type=jnp.float32)
        * score_scale
    )
    key_mask = inside[:, None, None, :, :]
    scores = jnp.where(key_mask, scores, -1e30)
    new_max = jnp.maximum(row_max, jnp.max(scores, axis=(3, 4)))
    weights = jnp.where(key_mask, jnp.exp(scores - new_max[..., None, None]), 0.0)
    shrink = jnp.exp(row_max - new_max)
    row_sum = jnp.sum(weights, axis=(3, 4))
    rounded = weights.astype(jnp.bfloat16)
    product = jnp.einsum(
        "qhblk,qlkhd->qhbd", rounded, value_rows, preferred_element_type=jnp.float32
    )
    accumulated = product
    return (new_max, row_sum, accumulated)


def body(queries, keys, values, live_blocks):
    tokens = queries.shape[0]
    share = H // KVH
    heads_here = H // lax.axis_size("uly")
    query_heads = queries.reshape(tokens, H, HD)
    key_heads = jnp.repeat(keys.reshape(tokens, KVH, HD), share, axis=1)
    value_heads = jnp.repeat(values.reshape(tokens, KVH, HD), share, axis=1)
    query_here, key_here, value_here = (
        lax.all_to_all(query_heads, "uly", split_axis=1, concat_axis=0, tiled=True),
        lax.all_to_all(key_heads, "uly", split_axis=1, concat_axis=0, tiled=True),
        lax.all_to_all(value_heads, "uly", split_axis=1, concat_axis=0, tiled=True),
    )
    length = query_here.shape[0]
    count_blocks = length // BLOCK
    first_block = lax.axis_index("blk") * count_blocks
    rows_live = lax.dynamic_slice_in_dim(live_blocks, first_block, count_blocks, 0)
    query_blocks = query_here.reshape(count_blocks, BLOCK, heads_here, HD)
    score_scale = 1.0 / math.sqrt(HD)
    start_state = (
        jnp.full((count_blocks, heads_here, BLOCK), -1e30, jnp.float32),
        jnp.zeros((count_blocks, heads_here, BLOCK), jnp.float32),
        jnp.zeros((count_blocks, heads_here, BLOCK, HD), jnp.float32),
    )
    fold_step = partial(
        attend_piece, query_blocks=query_blocks, rows_live=rows_live, score_scale=score_scale
    )
    whole_keys, whole_values = (
        lax.all_gather(key_here, "blk", axis=0, tiled=True),
        lax.all_gather(value_here, "blk", axis=0, tiled=True),
    )
    row_max, row_sum, accumulated = fold_step(start_state, (whole_keys, whole_values), 0)
    attended = (accumulated / row_sum[..., None]).astype(jnp.bfloat16)
    attended = attended.transpose(0, 2, 1, 3).reshape(length, heads_here, HD)
    regrouped = lax.all_to_all(attended, "uly", split_axis=0, concat_axis=1, tiled=True)
    return regrouped.reshape(tokens, H * HD)


def solution(mesh):
    return jax.shard_map(
        body,
        mesh=mesh,
        in_specs=(P(("blk", "uly"), None), P(("blk", "uly"), None), P(("blk", "uly"), None), P()),
        out_specs=P(("blk", "uly"), None),
        check_vma=False,
    )
```

profile of v0, /device:TPU:0, one launch (start us, length us, event | category | flops | bytes accessed | tf_op | source)
XLA Modules:
  0.0 267.9 jit_solution(3534199875093710729)
XLA Ops:
  6.5 1.1 copy_bitcast_fusion.2
  7.6 0.2 broadcast_in_dim.38
  7.9 32.9 %all_to_all.66 = bf16[128,32,128]{2,0,1:T(8,128)(2,1)S(1)} all-to-all(bf16[128,32,128]{2,0,1:T(8,128)(2,1)S(1)} %bitcast.68), channel_id=1, replica_groups=mesh['uly'=8,'blk'=4] {'uly'}, dimensions={1} | all-to-all | bytes 2097152 | tf_op jit(solution)/shard_map/all_to_all | solution.py:56
  40.8 0.1 copy.35
  40.9 1.8 copy.36
  42.8 0.2 broadcast_in_dim.42
  43.0 28.9 %all_to_all.67 = bf16[128,32,128]{2,0,1:T(8,128)(2,1)S(1)} all-to-all(bf16[128,32,128]{2,0,1:T(8,128)(2,1)S(1)} %bitcast.69), channel_id=1, replica_groups=mesh['uly'=8,'blk'=4] {'uly'}, dimensions={1} | all-to-all | bytes 2097152 | tf_op jit(solution)/shard_map/all_to_all | solution.py:57
  71.9 0.1 copy.42
  72.0 1.8 copy.43
  73.8 1.3 copy_bitcast_fusion
  75.1 3.6 %all-to-all-start.1 = ((bf16[128,32,128]{2,0,1:T(8,128)(2,1)}), bf16[128,32,128]{2,0,1:T(8,128)(2,1)S(1)}, u32[]{:S(2)}, u32[]{:S(2)}) async-start(bf16[128,32,128]{2,0,1:T(8,128)(2,1)} %copy_bitcast_fusion), calls=%async_computation.1 | async-start | bytes 2097152 | tf_op jit(solution)/shard_map/all_to_all | solution.py:55
  78.9 0.1 fusion.21
  79.1 58.5 %gather_fusion = bf16[8192,4,128]{2,1,0:T(4,128)(2,1)} fusion(bf16[4096,4,128]{2,1,0:T(4,128)(2,1)} %all-gather.3.cloned.1.call-done, s32[8192]{0:T(1024)S(1)} %fusion.21), kind=kCustom, calls=%fused_computation | custom fusion | bytes 16809984 | tf_op jit(solution)/shard_map/gather | solution.py:27
  137.6 8.3 %bitcast_reduce_fusion = (f32[8,4,128]{2,1,0:T(4,128)S(1)}, f32[8,4,8,128,128]{4,3,2,1,0:T(8,128)S(1)}) fusion(pred[8,8,128]{2,1,0:T(8,128)(4,1)S(1)} %fusion.24, bf16[8,128,4,128,1]{3,1,4,2,0:T(8,128)(2,1)S(1)} %bitcast.77, bf16[8,8,128,4,128]{4,3,2,1,0:T(4,128)(2,1)} %bitcast.66), kind=kOutput, calls=%fused_computation.3 | convolution fusion | flops 1086320640 | bytes 26238976 | tf_op jit(solution)/shard_map/qbhd,qlkhd->qhblk/dot_general | solution.py:30
  145.9 5.7 %copy-done.1 = f32[8,4,8,128,128]{4,3,2,1,0:T(8,128)} copy-done((f32[8,4,8,128,128]{4,3,2,1,0:T(8,128)}, f32[8,4,8,128,128]{4,3,2,1,0:T(8,128)S(1)}, u32[]{:S(2)}) %copy-start.1) | copy-done | bytes 16777240
  151.6 4.8 %fusion.2 = f32[8,4,128]{2,1,0:T(4,128)S(1)} fusion(f32[8,4,8,128,128]{4,3,2,1,0:T(8,128)S(1)} %get-tuple-element.6, f32[8,4,128]{2,1,0:T(4,128)S(1)} %broadcast_maximum_fusion, pred[8,8,128]{2,1,0:T(8,128)(4,1)S(1)} %fusion.24), kind=kLoop, calls=%fused_computation.7 | loop fusion | flops 20967424 | bytes 16818176 | tf_op jit(solution)/shard_map/reduce_sum | solution.py:38
  156.5 58.5 %gather_fusion.1 = bf16[8192,4,128]{2,1,0:T(4,128)(2,1)} fusion(bf16[4096,4,128]{2,1,0:T(4,128)(2,1)} %all-gather.5.cloned.1.call-done, s32[8192]{0:T(1024)S(1)} %fusion.21), kind=kCustom, calls=%fused_computation.1 | custom fusion | bytes 16809984 | tf_op jit(solution)/shard_map/gather | solution.py:28
  215.0 12.4 %fusion.15 = bf16[8,128,4,128]{3,1,2,0:T(8,128)(2,1)S(1)} fusion(bf16[8,8,128,4,128]{4,3,2,1,0:T(4,128)(2,1)} %bitcast.67, f32[8,4,8,128,128]{4,3,2,1,0:T(8,128)} %copy-done.1, f32[8,4,128]{2,1,0:T(4,128)S(1)} %broadcast_maximum_fusion, pred[8,8,128]{2,1,0:T(8,128)(4,1)S(1)} %fusion.24, f32[8,128,4]{1,2,0:T(4,128)S(1)} %bitcast.78), kind=kOutput, calls=%fused_computation.20 | convolution fusion | flops 1095761920 | bytes 26255360 | tf_op jit(solution)/shard_map/qhblk,qlkhd->qhbd/dot_general | solution.py:40
  227.4 0.1 copy.47
  227.5 0.8 copy.48
  228.4 30.6 %all_to_all.68 = bf16[1024,4,128]{2,1,0:T(4,128)(2,1)S(1)} all-to-all(bf16[1024,4,128]{2,1,0:T(4,128)(2,1)S(1)} %copy.48), channel_id=1, replica_groups=mesh['uly'=8,'blk'=4] {'uly'}, dimensions={0} | all-to-all | bytes 2097152 | tf_op jit(solution)/shard_map/all_to_all | solution.py:80
  258.9 0.1 copy.49
  259.1 0.7 copy.50
  259.8 1.3 copy.51
  (19 shorter events, 0.4 us)
Async XLA Ops:
  6.5 67.3 %copy-start = (bf16[128,4096]{1,0:T(8,128)(2,1)S(1)}, bf16[128,4096]{1,0:T(8,128)(2,1)}, u32[]{:S(2)}) copy-start(bf16[128,4096]{1,0:T(8,128)(2,1)} %param.4) | copy-start | bytes 3145732
  6.5 36.2 %copy-start.2 = (bf16[128,1024]{1,0:T(8,128)(2,1)S(1)}, bf16[128,1024]{1,0:T(8,128)(2,1)}, u32[]{:S(2)}) copy-start(bf16[128,1024]{1,0:T(8,128)(2,1)} %param.6) | copy-start | bytes 786436
  6.5 72.5 %all-gather.3.cloned.1.call-start = ((), (), s32[]{:S(2)}) async-start(), calls=%async_computation.4 | async-start | bytes 5242880 | tf_op jit(solution)/shard_map/all_gather | solution.py:74
  40.9 37.8 %copy-start.3 = (s32[32,8]{0,1:T(8,128)S(1)}, s32[32,8]{0,1:T(8,128)}, u32[]{:S(2)}) copy-start(s32[32,8]{0,1:T(8,128)} %param.7) | copy-start | bytes 3076
  42.7 113.8 %all-gather.5.cloned.1.call-start = ((), (), s32[]{:S(2)}) async-start(), calls=%async_computation.5 | async-start | bytes 5242880 | tf_op jit(solution)/shard_map/all_gather | solution.py:75
  75.1 62.5 %all-to-all-start.1 = ((bf16[128,32,128]{2,0,1:T(8,128)(2,1)}), bf16[128,32,128]{2,0,1:T(8,128)(2,1)S(1)}, u32[]{:S(2)}, u32[]{:S(2)}) async-start(bf16[128,32,128]{2,0,1:T(8,128)(2,1)} %copy_bitcast_fusion), calls=%async_computation.1 | async-start | bytes 2097152 | tf_op jit(solution)/shard_map/all_to_all | solution.py:55
  145.9 5.7 %copy-start.1 = (f32[8,4,8,128,128]{4,3,2,1,0:T(8,128)}, f32[8,4,8,128,128]{4,3,2,1,0:T(8,128)S(1)}, u32[]{:S(2)}) copy-start(f32[8,4,8,128,128]{4,3,2,1,0:T(8,128)S(1)} %get-tuple-element.6) | copy-start | bytes 50331652
Sparse Core Ops, SparseCore 0:
  42.8 33.4 all-gather.2
  77.8 34.4 all-gather.4
where the time goes:
time: 268 us
  local copies, waits for them, and re-layouts  133 us (50%)
  blocking collectives  92.3 us (34%)
  matrix products  20.7 us (8%)
  between operations  13.6 us (5%)
  other arithmetic  5.06 us (2%)
  starting transfers between devices  3.6 us (1%)
    gather x1, local copies, waits for them, and re-layouts, attend_piece(): value_rows = value_part[picked]  58.5 us
    gather x1, local copies, waits for them, and re-layouts, attend_piece(): key_rows = key_part[picked]  58.5 us
    all_to_all x1, blocking collectives, body(): lax.all_to_all(key_heads, 'uly', split_axis=1, concat_axis=0, tiled=True)  32.9 us
    all_to_all x1, blocking collectives, body(): lax.all_to_all(attended, 'uly', split_axis=0, concat_axis=1, tiled=True)  30.6 us
    all_to_all x1, blocking collectives, body(): lax.all_to_all(value_heads, 'uly', split_axis=1, concat_axis=0, tiled=True)  28.9 us
    dot_general x1, matrix products, attend_piece(): jnp.einsum('qhblk,qlkhd->qhbd', rounded, value_rows, preferred_element_ty...  12.4 us
    dot_general x1, matrix products, attend_piece(): jnp.einsum('qbhd,qlkhd->qhblk', query_blocks, key_rows, preferred_element...  8.3 us
    unnamed x8, local copies, waits for them, and re-layouts  5.72 us
  transfers between devices with their start and end apart: 3, of which 0 were waited for; matrix products, arithmetic and copies ran while one was open for 28% of the time, Pallas kernels for 0%

commit v1 on v0

v1 whole, which is shorter than its diff:
```python
import math

import jax
import jax.numpy as jnp
from jax import lax
from jax.experimental import pallas as pl
from jax.experimental.pallas import tpu as pltpu
from jax.sharding import PartitionSpec as P

HD = 128
CORES = 2
SIDE = 2
GROUP = SIDE * SIDE * CORES
MESH = pl.DeviceIdType.MESH


class Layout:
    def __init__(self, n_uly, n_blk):
        self.n_uly = n_uly
        self.nx = n_blk // CORES
        self.ny = 2 ** (int(math.log2(n_uly)) // 2)
        self.nz = n_uly // self.ny
        self.columns = n_uly * n_blk // GROUP

    def split(self, uly, blk):
        x, core = blk // CORES, blk % CORES
        z, y = uly // self.ny, uly % self.ny
        column = ((x // SIDE) * (self.ny // SIDE) + y // SIDE) * self.nz + z
        member = ((x % SIDE) * SIDE + y % SIDE) * CORES + core
        return column, member

    def join(self, column, member):
        z, square = column % self.nz, column // self.nz
        x = (square // (self.ny // SIDE)) * SIDE + member // (SIDE * CORES)
        y = (square % (self.ny // SIDE)) * SIDE + (member // CORES) % SIDE
        return z * self.ny + y, x * CORES + member % CORES

    def slot(self, block):
        column, member = self.split(block % self.n_uly, block // self.n_uly)
        return column * GROUP + member


def partner(member, rel):
    a = (member // 4 + rel // 4) % 2
    b = ((member // 2) % 2 + (rel // 2) % 2) % 2
    c = (member % 2 + rel % 2) % 2
    return a * 4 + b * 2 + c


def kernel(lay, live_ref, q_ref, k_ref, v_ref, o_ref,
           qbuf, kbuf, vbuf, pbuf, lbuf, obuf,
           plane_send, plane_recv, own_sem, relay_send, k_recv, v_recv, o_send, o_recv):
    width = q_ref.shape[1] // GROUP
    share = width // HD
    live = live_ref.shape[1]
    last = lay.columns - 1
    column, member = lay.split(lax.axis_index("uly"), lax.axis_index("blk"))

    def device(col, mem):
        uly, blk = lay.join(col, mem)
        return {"uly": uly, "blk": blk}

    has_down, has_up = column > 0, column < last
    down, up = jnp.maximum(column - 1, 0), jnp.minimum(column + 1, last)

    barrier = pltpu.get_barrier_semaphore()
    for rel in range(1, GROUP):
        pl.semaphore_signal(barrier, inc=1, device_id=device(column, partner(member, rel)), device_id_type=MESH)

    @pl.when(has_down)
    def _():
        pl.semaphore_signal(barrier, inc=1, device_id=device(down, member), device_id_type=MESH)

    @pl.when(has_up)
    def _():
        pl.semaphore_signal(barrier, inc=1, device_id=device(up, member), device_id_type=MESH)

    def cols(index, size):
        return pl.ds(pl.multiple_of(index * size, size), size)

    here = column * GROUP + member
    own = [
        pltpu.make_async_copy(k_ref.at[:, cols(member, HD)], kbuf.at[here], own_sem.at[0]),
        pltpu.make_async_copy(v_ref.at[:, cols(member, HD)], vbuf.at[here], own_sem.at[1]),
        pltpu.make_async_copy(q_ref.at[:, cols(member, width)], qbuf.at[0], own_sem.at[2]),
    ]
    for copy in own:
        copy.start()
    arrivals = 7 + has_down.astype(jnp.int32) + has_up.astype(jnp.int32)
    pl.semaphore_wait(barrier, arrivals)

    def plane(kind, rel, source_member=None):
        other = partner(member, rel)
        src, dst, size = (
            (k_ref, kbuf.at[here], HD),
            (v_ref, vbuf.at[here], HD),
            (q_ref, qbuf.at[rel], width),
        )[kind]
        return pltpu.make_async_remote_copy(
            src.at[:, cols(other, size)], dst, plane_send.at[kind, rel], plane_recv.at[kind, rel],
            device_id=device(column, other), device_id_type=MESH,
        )

    for kind in range(3):
        for rel in range(1, GROUP):
            plane(kind, rel).start()

    def hop(kind, way, col, item):
        buf, recv = ((kbuf, k_recv), (vbuf, v_recv))[kind]
        index = col * GROUP + item
        return pltpu.make_async_remote_copy(
            buf.at[index], buf.at[index], relay_send.at[kind, way, col], recv.at[index],
            device_id=device((down, up)[way], member), device_id_type=MESH,
        )

    def forward(kind, way, col, item):
        @pl.when((has_down, has_up)[way])
        def _():
            hop(kind, way, col, item).start()

    for kind in range(2):
        for rel in range(GROUP):
            if rel == 0:
                own[kind].wait()
            else:
                plane(kind, rel).wait_recv()
            forward(kind, 0, column, partner(member, rel))
            forward(kind, 1, column, partner(member, rel))

    @pl.loop(1, lay.columns)
    def _(step):
        above, below = column + step, column - step
        for kind in range(2):
            @pl.loop(0, GROUP)
            def _(item):
                @pl.when((above <= last) if kind == 0 else ((above <= last) & has_down))
                def _():
                    hop(kind, 0, above, item).wait_recv()
                    forward(kind, 0, above, item)

                @pl.when((below >= 0) if kind == 0 else ((below >= 0) & has_up))
                def _():
                    hop(kind, 1, below, item).wait_recv()
                    forward(kind, 1, below, item)

    own[2].wait()
    for rel in range(1, GROUP):
        plane(2, rel).wait_recv()

    factor = math.log2(math.e) / math.sqrt(HD)

    def block_of(rel):
        uly, blk = lay.join(column, partner(member, rel))
        return blk * lay.n_uly + uly

    def picked(buf, rel):
        block = block_of(rel)
        return jnp.concatenate([buf[lay.slot(live_ref[block, i])] for i in range(live)], axis=0)

    @pl.loop(0, GROUP)
    def _(rel):
        queries = jnp.concatenate([qbuf[rel, :, r * HD:(r + 1) * HD] for r in range(share)], axis=0)
        scores = lax.dot_general(
            queries, picked(kbuf, rel), (((1,), (1,)), ((), ())), preferred_element_type=jnp.float32
        )
        row_max = jnp.max(scores, axis=1, keepdims=True)
        weights = jnp.exp2((scores - row_max) * factor)
        total = jnp.sum(weights, axis=1, keepdims=True)
        lbuf[rel] = jnp.broadcast_to(total, lbuf.shape[1:])
        pbuf[rel] = weights.astype(jnp.bfloat16)

    @pl.loop(1, lay.columns)
    def _(step):
        above, below = column + step, column - step

        @pl.loop(0, GROUP)
        def _(item):
            @pl.when((above <= last) & jnp.logical_not(has_down))
            def _():
                hop(1, 0, above, item).wait_recv()

            @pl.when((below >= 0) & jnp.logical_not(has_up))
            def _():
                hop(1, 1, below, item).wait_recv()

    def back(rel):
        other = partner(member, rel)
        return pltpu.make_async_remote_copy(
            obuf.at[rel], o_ref.at[:, cols(member, width)], o_send.at[rel], o_recv.at[rel],
            device_id=device(column, other), device_id_type=MESH,
        )

    def attended(rel):
        product = jnp.dot(pbuf[rel], picked(vbuf, rel), preferred_element_type=jnp.float32)
        result = (product / lbuf[rel]).astype(jnp.bfloat16)
        rows = result.shape[0] // share
        return jnp.concatenate([result[r * rows:(r + 1) * rows] for r in range(share)], axis=1)

    @pl.loop(0, GROUP - 1)
    def _(step):
        rel = GROUP - 1 - step
        obuf[rel] = attended(rel)

        @pl.when(step > 0)
        def _():
            back(rel + 1).start()

    o_ref[:, cols(member, width)] = attended(0)
    back(1).start()

    for kind in range(3):
        for rel in range(1, GROUP):
            plane(kind, rel).wait_send()

    def sent(kind, way, col):
        buf = (kbuf, vbuf)[kind].at[pl.ds(col * GROUP, GROUP)]
        pltpu.make_async_copy(buf, buf, relay_send.at[kind, way, col]).wait()

    @pl.loop(0, lay.columns)
    def _(col):
        for kind in range(2):
            @pl.when((col >= column) & has_down)
            def _():
                sent(kind, 0, col)

            @pl.when((col <= column) & has_up)
            def _():
                sent(kind, 1, col)

    for rel in range(1, GROUP):
        back(rel).wait()


def solution(mesh):
    lay = Layout(mesh.shape["uly"], mesh.shape["blk"])

    def body(queries, keys, values, live_blocks):
        rows, hidden = queries.shape
        width = hidden // GROUP
        share = width // HD
        slots = lay.columns * GROUP
        keys_seen = live_blocks.shape[1] * rows
        bf16, f32 = jnp.bfloat16, jnp.float32
        dma = pltpu.SemaphoreType.DMA
        vmem = pl.BlockSpec(memory_space=pltpu.VMEM)

        def call(*refs):
            kernel(lay, *refs)

        return pl.pallas_call(
            call,
            out_shape=jax.ShapeDtypeStruct((rows, hidden), bf16),
            in_specs=[pl.BlockSpec(memory_space=pltpu.SMEM), vmem, vmem, vmem],
            out_specs=vmem,
            scratch_shapes=[
                pltpu.VMEM((GROUP, rows, width), bf16),
                pltpu.VMEM((slots, rows, HD), bf16),
                pltpu.VMEM((slots, rows, HD), bf16),
                pltpu.VMEM((GROUP, rows * share, keys_seen), bf16),
                pltpu.VMEM((GROUP, rows * share, HD), f32),
                pltpu.VMEM((GROUP, rows, width), bf16),
                dma((3, GROUP)),
                dma((3, GROUP)),
                dma((3,)),
                dma((2, 2, lay.columns)),
                dma((slots,)),
                dma((slots,)),
                dma((GROUP,)),
                dma((GROUP,)),
            ],
            compiler_params=pltpu.CompilerParams(
                collective_id=0, has_side_effects=True, vmem_limit_bytes=56 * 2**20
            ),
            name="group_attention",
        )(live_blocks, queries, keys, values)

    spec = P(("blk", "uly"), None)
    return jax.shard_map(
        body, mesh=mesh, in_specs=(spec, spec, spec, P()), out_specs=spec, check_vma=False
    )
```

time: 268 us -> 66.8 us (0.25)
  local copies, waits for them, and re-layouts: 133 us -> 3.65 us
  blocking collectives: 92.3 us -> 0 us
  Pallas kernels: 0 us -> 62.9 us
  matrix products: 20.7 us -> 0 us
  between operations: 13.6 us -> 0.01 us
  other arithmetic: 5.06 us -> 0 us
  starting transfers between devices: 3.6 us -> 0 us
    gather x2 -> x0, local copies, waits for them, and re-layouts: 117 us -> none  [the longest x1 58.5 us: attend_piece(): value_rows = value_part[picked]]
    all_to_all x3 -> x0, blocking collectives: 92.3 us -> none  [the longest x1 32.9 us: body(): lax.all_to_all(key_heads, 'uly', split_axis=1, concat_axis=0, tiled=True)]
    pallas_call x0 -> x1, Pallas kernels: none -> 62.9 us  [body(): pl.pallas_call(call, out_shape=jax.ShapeDtypeStruct((rows, hidden), bf16)...]
    dot_general x2 -> x0, matrix products: 20.7 us -> none  [the longest x1 12.4 us: attend_piece(): jnp.einsum('qhblk,qlkhd->qhbd', rounded, value_rows, preferred_element_ty...]
    reduce_sum x1 -> x0, other arithmetic: 4.81 us -> none  [attend_piece(): row_sum = jnp.sum(weights, axis=(3, 4))]
    reshape x5 -> x0, local copies, waits for them, and re-layouts: 4.6 us -> none  [the longest x1 1.33 us: body(): query_heads = queries.reshape(tokens, H, HD)]
    all_to_all x6 -> x0, local copies, waits for them, and re-layouts: 4.56 us -> none  [the longest x2 1.88 us: body(): lax.all_to_all(value_heads, 'uly', split_axis=1, concat_axis=0, tiled=True)]
    all_to_all x1 -> x0, starting transfers between devices: 3.56 us -> none  [body(): lax.all_to_all(query_heads, 'uly', split_axis=1, concat_axis=0, tiled=True)]
  transfers between devices with their start and end apart: 3 -> 0, of which waited for: 0 -> 0; matrix products, arithmetic and copies ran while one was open for 28% -> 0% of each run, Pallas kernels for 0% -> 0%
where the time goes in v1:
time: 66.8 us; the launch traced here: 66.6 us
  Pallas kernels  62.9 us (94%)
  local copies, waits for them, and re-layouts  3.65 us (5%)
    pallas_call x1, Pallas kernels, body(): pl.pallas_call(call, out_shape=jax.ShapeDtypeStruct((rows, hidden), bf16)...  62.9 us
    unnamed x2, local copies, waits for them, and re-layouts  3.65 us

profile of v1, /device:TPU:0, one launch (start us, length us, event | category | flops | bytes accessed | tf_op | source)
XLA Modules:
  0.0 66.6 jit_solution(12674089444249157628)
XLA Ops:
  0.0 1.4 %copy.5.refs_0_ = s32[32,8]{1,0:T(8,128)} copy(s32[32,8]{0,1:T(8,128)} %param.7) | data formatting | bytes 2048 | tf_op args[3]
  1.4 62.9 %group_attention.1 = bf16[128,4096]{1,0:T(8,128)(2,1)} custom-call(s32[32,8]{1,0:T(8,128)} %copy.5.refs_0_, bf16[128,4096]{1,0:T(8,128)(2,1)} %refs_1_.1, bf16[128,1024]{1,0:T(8,128)(2,1)} %refs_2_.1, bf16[128,1024]{1,0:T(8,128)(2,1)} %refs_3_.1), custom_call_target="tpu_custom_call" | custom-call | tf_op jit(solution)/shard_map/group_attention/pallas_call | solution.py:250
  64.3 2.3 %copy.7 = bf16[128,4096]{1,0:T(8,128)(2,1)} copy(bf16[128,4096]{1,0:T(8,128)(2,1)} %group_attention.1) | data formatting | bytes 2097152

commit v2 on v1

v2 whole, which is shorter than its diff:
```python
import math

import jax
import jax.numpy as jnp
from jax import lax
from jax.experimental import pallas as pl
from jax.experimental.pallas import tpu as pltpu
from jax.sharding import PartitionSpec as P

HD = 128
CORES = 2
SIDE = 2
CHIPS = SIDE * SIDE
GROUP = CHIPS * CORES
MESH = pl.DeviceIdType.MESH


class Layout:
    def __init__(self, n_uly, n_blk):
        self.n_uly = n_uly
        self.nx = n_blk // CORES
        self.ny = 2 ** (int(math.log2(n_uly)) // 2)
        self.nz = n_uly // self.ny
        self.columns = n_uly * n_blk // GROUP

    def split(self, uly, blk):
        x, core = blk // CORES, blk % CORES
        z, y = uly // self.ny, uly % self.ny
        column = ((x // SIDE) * (self.ny // SIDE) + y // SIDE) * self.nz + z
        return column, (x % SIDE) * SIDE + y % SIDE, core

    def join(self, column, chip, core):
        z, square = column % self.nz, column // self.nz
        x = (square // (self.ny // SIDE)) * SIDE + chip // SIDE
        y = (square % (self.ny // SIDE)) * SIDE + chip % SIDE
        return z * self.ny + y, x * CORES + core

    def slot(self, block):
        column, chip, core = self.split(block % self.n_uly, block // self.n_uly)
        return column * GROUP + core * CHIPS + chip


def partner(chip, rel):
    a = (chip // 2 + rel // 2) % 2
    b = (chip % 2 + rel % 2) % 2
    return a * 2 + b


def kernel(lay, live_ref, q_ref, k_ref, v_ref, o_ref,
           qbuf, ka, va, kb, vb, pbuf, lbuf, obuf,
           plane_send, plane_recv, own_sem, relay_send, recv, o_send, o_recv):
    heads = k_ref.shape[1] // HD // CHIPS
    width = q_ref.shape[1] // CHIPS // heads
    share = width // HD
    live = live_ref.shape[1]
    last = lay.columns - 1
    bufs = ((ka, va), (kb, vb))
    column, chip, core = lay.split(lax.axis_index("uly"), lax.axis_index("blk"))

    def device(col, which, core_of):
        uly, blk = lay.join(col, which, core_of)
        return {"uly": uly, "blk": blk}

    has_down, has_up = column > 0, column < last
    middle = has_down & has_up
    down, up = jnp.maximum(column - 1, 0), jnp.minimum(column + 1, last)
    targets = (device(down, chip, core), device(up, chip, core), device(column, chip, 1 - core))

    barrier = pltpu.get_barrier_semaphore()
    for rel in range(1, CHIPS):
        pl.semaphore_signal(
            barrier, inc=1, device_id=device(column, partner(chip, rel), core), device_id_type=MESH
        )
    pl.semaphore_signal(barrier, inc=1, device_id=targets[2], device_id_type=MESH)

    @pl.when(has_down)
    def _():
        pl.semaphore_signal(barrier, inc=1, device_id=targets[0], device_id_type=MESH)

    @pl.when(has_up)
    def _():
        pl.semaphore_signal(barrier, inc=1, device_id=targets[1], device_id_type=MESH)

    def cols(index, size):
        return pl.ds(pl.multiple_of(index * size, size), size)

    def slot_of(col, item, core_of):
        return col * GROUP + core_of * CHIPS + item

    here = slot_of(column, chip, core)

    def route(head, kind, rel):
        src, dst, size = (
            (k_ref, bufs[head][0].at[here], HD),
            (v_ref, bufs[head][1].at[here], HD),
            (q_ref, qbuf.at[head, rel], width),
        )[kind]
        return src.at[:, cols(partner(chip, rel) * heads + head, size)], dst

    def own(head, kind):
        src, dst = route(head, kind, 0)
        return pltpu.make_async_copy(src, dst, own_sem.at[head, kind])

    def plane(head, kind, rel):
        src, dst = route(head, kind, rel)
        return pltpu.make_async_remote_copy(
            src, dst, plane_send.at[head, kind, rel], plane_recv.at[head, kind, rel],
            device_id=device(column, partner(chip, rel), core), device_id_type=MESH,
        )

    for head in range(heads):
        for kind in range(3):
            own(head, kind).start()
    pl.semaphore_wait(barrier, CHIPS + has_down.astype(jnp.int32) + has_up.astype(jnp.int32))
    for head in range(heads):
        for kind in range(3):
            for rel in range(1, CHIPS):
                plane(head, kind, rel).start()

    def hop(head, kind, way, col, item, core_of):
        buf = bufs[head][kind]
        index = slot_of(col, item, core_of)
        return pltpu.make_async_remote_copy(
            buf.at[index], buf.at[index], relay_send.at[head, kind, way, col], recv.at[head, kind, index],
            device_id=targets[way], device_id_type=MESH,
        )

    def first(head):
        for kind in range(2):
            for rel in range(CHIPS):
                if rel == 0:
                    own(head, kind).wait()
                else:
                    plane(head, kind, rel).wait_recv()

                @pl.when(has_down)
                def _():
                    hop(head, kind, 0, column, partner(chip, rel), core).start()

                @pl.when(has_up)
                def _():
                    hop(head, kind, 1, column, partner(chip, rel), core).start()

                hop(head, kind, 2, column, partner(chip, rel), core).start()

    def relay(head):
        @pl.loop(1, lay.columns)
        def _(step):
            above, below = column + step, column - step
            for kind in range(2):
                @pl.loop(0, CHIPS)
                def _(item):
                    @pl.when((above <= last) & has_down)
                    def _():
                        hop(head, kind, 0, above, item, core).wait_recv()
                        hop(head, kind, 0, above, item, core).start()
                        hop(head, kind, 2, above, item, core).start()

                    @pl.when((below >= 0) & has_up)
                    def _():
                        hop(head, kind, 1, below, item, core).wait_recv()
                        hop(head, kind, 1, below, item, core).start()
                        hop(head, kind, 2, below, item, core).start()

    def finish(head, kind):
        @pl.loop(1, lay.columns)
        def _(step):
            above, below = column + step, column - step

            @pl.loop(0, CHIPS)
            def _(item):
                @pl.when((above <= last) & jnp.logical_not(has_down))
                def _():
                    hop(head, kind, 0, above, item, core).wait_recv()
                    hop(head, kind, 2, above, item, core).start()

                @pl.when((below >= 0) & jnp.logical_not(has_up))
                def _():
                    hop(head, kind, 1, below, item, core).wait_recv()
                    hop(head, kind, 2, below, item, core).start()

        @pl.loop(0, lay.columns)
        def _(col):
            @pl.loop(0, CHIPS)
            def _(item):
                hop(head, kind, 2, col, item, 1 - core).wait_recv()

    factor = math.log2(math.e) / math.sqrt(HD)

    def picked(buf, rel):
        uly, blk = lay.join(column, partner(chip, rel), core)
        block = blk * lay.n_uly + uly
        return jnp.concatenate([buf[lay.slot(live_ref[block, i])] for i in range(live)], axis=0)

    def weigh(head):
        own(head, 2).wait()
        for rel in range(1, CHIPS):
            plane(head, 2, rel).wait_recv()

        @pl.loop(0, CHIPS)
        def _(rel):
            queries = jnp.concatenate(
                [qbuf[head, rel, :, r * HD:(r + 1) * HD] for r in range(share)], axis=0
            )
            scores = lax.dot_general(
                queries, picked(bufs[head][0], rel), (((1,), (1,)), ((), ())),
                preferred_element_type=jnp.float32,
            )
            row_max = jnp.max(scores, axis=1, keepdims=True)
            weights = jnp.exp2((scores - row_max) * factor)
            total = jnp.sum(weights, axis=1, keepdims=True)
            lbuf[rel] = jnp.broadcast_to(total, lbuf.shape[1:])
            pbuf[rel] = weights.astype(jnp.bfloat16)

    def out_cols(head):
        return cols(chip * heads + head, width)

    def back(head, rel):
        return pltpu.make_async_remote_copy(
            obuf.at[head, rel], o_ref.at[:, out_cols(head)], o_send.at[head, rel], o_recv.at[head, rel],
            device_id=device(column, partner(chip, rel), core), device_id_type=MESH,
        )

    def attended(head, rel):
        product = jnp.dot(pbuf[rel], picked(bufs[head][1], rel), preferred_element_type=jnp.float32)
        result = (product / lbuf[rel]).astype(jnp.bfloat16)
        rows = result.shape[0] // share
        return jnp.concatenate([result[r * rows:(r + 1) * rows] for r in range(share)], axis=1)

    def attend(head):
        @pl.loop(0, CHIPS - 1)
        def _(step):
            rel = CHIPS - 1 - step
            obuf[head, rel] = attended(head, rel)

            @pl.when(step > 0)
            def _():
                back(head, rel + 1).start()

        o_ref[:, out_cols(head)] = attended(head, 0)
        back(head, 1).start()

    first(0)

    @pl.when(jnp.logical_not(middle))
    def _():
        for head in range(1, heads):
            first(head)

    relay(0)

    @pl.when(middle)
    def _():
        for head in range(1, heads):
            first(head)

    for head in range(1, heads):
        relay(head)
    for head in range(heads):
        finish(head, 0)
        weigh(head)
        finish(head, 1)
        attend(head)

    for head in range(heads):
        for kind in range(3):
            for rel in range(1, CHIPS):
                plane(head, kind, rel).wait_send()

    def sent(head, kind, way, col):
        buf = bufs[head][kind].at[pl.ds(slot_of(col, 0, core), CHIPS)]
        pltpu.make_async_copy(buf, buf, relay_send.at[head, kind, way, col]).wait()

    @pl.loop(0, lay.columns)
    def _(col):
        for head in range(heads):
            for kind in range(2):
                @pl.when((col >= column) & has_down)
                def _():
                    sent(head, kind, 0, col)

                @pl.when((col <= column) & has_up)
                def _():
                    sent(head, kind, 1, col)

                sent(head, kind, 2, col)

    for head in range(heads):
        for rel in range(1, CHIPS):
            back(head, rel).wait()


def solution(mesh):
    lay = Layout(mesh.shape["uly"], mesh.shape["blk"])

    def body(queries, keys, values, live_blocks):
        rows, hidden = queries.shape
        heads = keys.shape[1] // HD // CHIPS
        width = hidden // CHIPS // heads
        share = width // HD
        slots = lay.columns * GROUP
        keys_seen = live_blocks.shape[1] * rows
        bf16, f32 = jnp.bfloat16, jnp.float32
        dma = pltpu.SemaphoreType.DMA
        vmem = pl.BlockSpec(memory_space=pltpu.VMEM)

        def call(*refs):
            kernel(lay, *refs)

        return pl.pallas_call(
            call,
            out_shape=jax.ShapeDtypeStruct((rows, hidden), bf16),
            in_specs=[pl.BlockSpec(memory_space=pltpu.SMEM), vmem, vmem, vmem],
            out_specs=vmem,
            scratch_shapes=[
                pltpu.VMEM((heads, CHIPS, rows, width), bf16),
                *[pltpu.VMEM((slots, rows, HD), bf16) for _ in range(4)],
                pltpu.VMEM((CHIPS, rows * share, keys_seen), bf16),
                pltpu.VMEM((CHIPS, rows * share, HD), f32),
                pltpu.VMEM((heads, CHIPS, rows, width), bf16),
                dma((heads, 3, CHIPS)),
                dma((heads, 3, CHIPS)),
                dma((heads, 3)),
                dma((heads, 2, 3, lay.columns)),
                dma((heads, 2, slots)),
                dma((heads, CHIPS)),
                dma((heads, CHIPS)),
            ],
            compiler_params=pltpu.CompilerParams(
                collective_id=0, has_side_effects=True, vmem_limit_bytes=56 * 2**20
            ),
            name="group_attention",
        )(live_blocks, queries, keys, values)

    spec = P(("blk", "uly"), None)
    return jax.shard_map(
        body, mesh=mesh, in_specs=(spec, spec, spec, P()), out_specs=spec, check_vma=False
    )
```

time: 66.8 us -> 62.8 us (0.940)
  Pallas kernels: 62.9 us -> 59 us
    pallas_call x1, Pallas kernels: 62.9 us -> 59 us  [body(): pl.pallas_call(call, out_shape=jax.ShapeDtypeStruct((rows, hidden), bf16)...]
where the time goes in v2:
time: 62.8 us; the launch traced here: 62.6 us
  Pallas kernels  59 us (94%)
  local copies, waits for them, and re-layouts  3.65 us (6%)
    pallas_call x1, Pallas kernels, body(): pl.pallas_call(call, out_shape=jax.ShapeDtypeStruct((rows, hidden), bf16)...  59 us
    unnamed x2, local copies, waits for them, and re-layouts  3.65 us

profile of v2, /device:TPU:0, one launch (start us, length us, event | category | flops | bytes accessed | tf_op | source)
XLA Modules:
  0.0 62.6 jit_solution(10376839867852376704)
XLA Ops:
  0.0 1.4 %copy.5.refs_0_ = s32[32,8]{1,0:T(8,128)} copy(s32[32,8]{0,1:T(8,128)} %param.7) | data formatting | bytes 2048 | tf_op args[3]
  1.4 59.0 %group_attention.1 = bf16[128,4096]{1,0:T(8,128)(2,1)} custom-call(s32[32,8]{1,0:T(8,128)} %copy.5.refs_0_, bf16[128,4096]{1,0:T(8,128)(2,1)} %refs_1_.1, bf16[128,1024]{1,0:T(8,128)(2,1)} %refs_2_.1, bf16[128,1024]{1,0:T(8,128)(2,1)} %refs_3_.1), custom_call_target="tpu_custom_call" | custom-call | tf_op jit(solution)/shard_map/group_attention/pallas_call | solution.py:310
  60.3 2.3 %copy.7 = bf16[128,4096]{1,0:T(8,128)(2,1)} copy(bf16[128,4096]{1,0:T(8,128)(2,1)} %group_attention.1) | data formatting | bytes 2097152

commit v3 on v2

--- a/solution.py
+++ b/solution.py
@@ -46,8 +46,8 @@
     return a * 2 + b
 
 
-def kernel(lay, live_ref, q_ref, k_ref, v_ref, o_ref,
-           qbuf, ka, va, kb, vb, pbuf, lbuf, obuf,
+def kernel(lay, live_hbm, q_ref, k_ref, v_ref, o_ref,
+           live_ref, live_sem, qbuf, ka, va, kb, vb, pbuf, lbuf, obuf,
            plane_send, plane_recv, own_sem, relay_send, recv, o_send, o_recv):
     heads = k_ref.shape[1] // HD // CHIPS
     width = q_ref.shape[1] // CHIPS // heads
@@ -66,6 +66,8 @@
     down, up = jnp.maximum(column - 1, 0), jnp.minimum(column + 1, last)
     targets = (device(down, chip, core), device(up, chip, core), device(column, chip, 1 - core))
 
+    fetch = pltpu.make_async_copy(live_hbm, live_ref, live_sem)
+    fetch.start()
     barrier = pltpu.get_barrier_semaphore()
     for rel in range(1, CHIPS):
         pl.semaphore_signal(
@@ -144,10 +146,11 @@
                 hop(head, kind, 2, column, partner(chip, rel), core).start()
 
     def relay(head):
-        @pl.loop(1, lay.columns)
-        def _(step):
-            above, below = column + step, column - step
-            for kind in range(2):
+        for kind in range(2):
+            @pl.loop(1, lay.columns)
+            def _(step):
+                above, below = column + step, column - step
+
                 @pl.loop(0, CHIPS)
                 def _(item):
                     @pl.when((above <= last) & has_down)
@@ -241,6 +244,7 @@
         back(head, 1).start()
 
     first(0)
+    fetch.wait()
 
     @pl.when(jnp.logical_not(middle))
     def _():
@@ -254,9 +258,9 @@
         for head in range(1, heads):
             first(head)
 
-    for head in range(1, heads):
-        relay(head)
-    for head in range(heads):
+    for head in range(heads):
+        if head > 0:
+            relay(head)
         finish(head, 0)
         weigh(head)
         finish(head, 1)
@@ -302,7 +306,6 @@
         keys_seen = live_blocks.shape[1] * rows
         bf16, f32 = jnp.bfloat16, jnp.float32
         dma = pltpu.SemaphoreType.DMA
-        vmem = pl.BlockSpec(memory_space=pltpu.VMEM)
 
         def call(*refs):
             kernel(lay, *refs)
@@ -310,9 +313,11 @@
         return pl.pallas_call(
             call,
             out_shape=jax.ShapeDtypeStruct((rows, hidden), bf16),
-            in_specs=[pl.BlockSpec(memory_space=pltpu.SMEM), vmem, vmem, vmem],
-            out_specs=vmem,
+            in_specs=[pl.BlockSpec(memory_space=pl.ANY)] * 4,
+            out_specs=pl.BlockSpec(memory_space=pltpu.VMEM),
             scratch_shapes=[
+                pltpu.SMEM(live_blocks.shape, live_blocks.dtype),
+                dma,
                 pltpu.VMEM((heads, CHIPS, rows, width), bf16),
                 *[pltpu.VMEM((slots, rows, HD), bf16) for _ in range(4)],
                 pltpu.VMEM((CHIPS, rows * share, keys_seen), bf16),

time: 62.8 us -> 59.9 us (0.954)
  Pallas kernels: 59 us -> 56.1 us
    pallas_call x1, Pallas kernels: 59 us -> 56.1 us  [body(): pl.pallas_call(call, out_shape=jax.ShapeDtypeStruct((rows, hidden), bf16)...]
where the time goes in v3:
time: 59.9 us; the launch traced here: 59.8 us
  Pallas kernels  56.1 us (94%)
  local copies, waits for them, and re-layouts  3.65 us (6%)
    pallas_call x1, Pallas kernels, body(): pl.pallas_call(call, out_shape=jax.ShapeDtypeStruct((rows, hidden), bf16)...  56.1 us
    unnamed x2, local copies, waits for them, and re-layouts  3.65 us

profile of v3, /device:TPU:0, one launch (start us, length us, event | category | flops | bytes accessed | tf_op | source)
XLA Modules:
  0.0 59.8 jit_solution(16436044131430406262)
XLA Ops:
  0.0 1.4 %copy.5.refs_0_ = s32[32,8]{1,0:T(8,128)} copy(s32[32,8]{0,1:T(8,128)} %param.7) | data formatting | bytes 2048 | tf_op args[3]
  1.4 56.1 %group_attention.1 = bf16[128,4096]{1,0:T(8,128)(2,1)} custom-call(s32[32,8]{1,0:T(8,128)} %copy.5.refs_0_, bf16[128,4096]{1,0:T(8,128)(2,1)} %refs_1_.1, bf16[128,1024]{1,0:T(8,128)(2,1)} %refs_2_.1, bf16[128,1024]{1,0:T(8,128)(2,1)} %refs_3_.1), custom_call_target="tpu_custom_call" | custom-call | tf_op jit(solution)/shard_map/group_attention/pallas_call | solution.py:313
  57.5 2.3 %copy.7 = bf16[128,4096]{1,0:T(8,128)(2,1)} copy(bf16[128,4096]{1,0:T(8,128)(2,1)} %group_attention.1) | data formatting | bytes 2097152

commit v4 on v3

--- a/solution.py
+++ b/solution.py
@@ -215,33 +215,45 @@
             lbuf[rel] = jnp.broadcast_to(total, lbuf.shape[1:])
             pbuf[rel] = weights.astype(jnp.bfloat16)
 
-    def out_cols(head):
-        return cols(chip * heads + head, width)
-
-    def back(head, rel):
+    def halves(part):
+        return pl.ds(part * (width // 2), width // 2)
+
+    def out_cols(head, part):
+        return cols((chip * heads + head) * 2 + part, width // 2)
+
+    def back(head, rel, part):
         return pltpu.make_async_remote_copy(
-            obuf.at[head, rel], o_ref.at[:, out_cols(head)], o_send.at[head, rel], o_recv.at[head, rel],
+            obuf.at[head, rel, :, halves(part)], o_ref.at[:, out_cols(head, part)],
+            o_send.at[head, rel, part], o_recv.at[head, rel, part],
             device_id=device(column, partner(chip, rel), core), device_id_type=MESH,
         )
 
-    def attended(head, rel):
-        product = jnp.dot(pbuf[rel], picked(bufs[head][1], rel), preferred_element_type=jnp.float32)
-        result = (product / lbuf[rel]).astype(jnp.bfloat16)
-        rows = result.shape[0] // share
-        return jnp.concatenate([result[r * rows:(r + 1) * rows] for r in range(share)], axis=1)
+    def attended(rel, part, values_here):
+        rows = pbuf.shape[1] // share
+        picks = pl.ds(part * (pbuf.shape[1] // 2), pbuf.shape[1] // 2)
+        product = jnp.dot(pbuf[rel, picks, :], values_here, preferred_element_type=jnp.float32)
+        result = (product / lbuf[rel, picks, :]).astype(jnp.bfloat16)
+        return jnp.concatenate([result[r * rows:(r + 1) * rows] for r in range(share // 2)], axis=1)
 
     def attend(head):
         @pl.loop(0, CHIPS - 1)
         def _(step):
             rel = CHIPS - 1 - step
-            obuf[head, rel] = attended(head, rel)
-
-            @pl.when(step > 0)
-            def _():
-                back(head, rel + 1).start()
-
-        o_ref[:, out_cols(head)] = attended(head, 0)
-        back(head, 1).start()
+            values_here = picked(bufs[head][1], rel)
+            for part in range(2):
+                obuf[head, rel, :, halves(part)] = attended(rel, part, values_here)
+                if part == 1:
+                    back(head, rel, 0).start()
+                else:
+                    @pl.when(step > 0)
+                    def _():
+                        back(head, rel + 1, 1).start()
+
+        values_here = picked(bufs[head][1], 0)
+        for part in range(2):
+            o_ref[:, out_cols(head, part)] = attended(0, part, values_here)
+            if part == 0:
+                back(head, 1, 1).start()
 
     first(0)
     fetch.wait()
@@ -291,7 +303,8 @@
 
     for head in range(heads):
         for rel in range(1, CHIPS):
-            back(head, rel).wait()
+            for part in range(2):
+                back(head, rel, part).wait()
 
 
 def solution(mesh):
@@ -328,8 +341,8 @@
                 dma((heads, 3)),
                 dma((heads, 2, 3, lay.columns)),
                 dma((heads, 2, slots)),
-                dma((heads, CHIPS)),
-                dma((heads, CHIPS)),
+                dma((heads, CHIPS, 2)),
+                dma((heads, CHIPS, 2)),
             ],
             compiler_params=pltpu.CompilerParams(
                 collective_id=0, has_side_effects=True, vmem_limit_bytes=56 * 2**20

time: 59.9 us -> 60 us (level)
  no operation moved by 1% of the time
where the time goes in v4:
time: 60 us; the launch traced here: 59.8 us
  Pallas kernels  56.2 us (94%)
  local copies, waits for them, and re-layouts  3.65 us (6%)
    pallas_call x1, Pallas kernels, body(): pl.pallas_call(call, out_shape=jax.ShapeDtypeStruct((rows, hidden), bf16)...  56.2 us
    unnamed x2, local copies, waits for them, and re-layouts  3.65 us

profile of v4, /device:TPU:0, one launch (start us, length us, event | category | flops | bytes accessed | tf_op | source)
XLA Modules:
  0.0 59.8 jit_solution(11429976432410389790)
XLA Ops:
  0.0 1.4 %copy.5.refs_0_ = s32[32,8]{1,0:T(8,128)} copy(s32[32,8]{0,1:T(8,128)} %param.7) | data formatting | bytes 2048 | tf_op args[3]
  1.4 56.2 %group_attention.1 = bf16[128,4096]{1,0:T(8,128)(2,1)} custom-call(s32[32,8]{1,0:T(8,128)} %copy.5.refs_0_, bf16[128,4096]{1,0:T(8,128)(2,1)} %refs_1_.1, bf16[128,1024]{1,0:T(8,128)(2,1)} %refs_2_.1, bf16[128,1024]{1,0:T(8,128)(2,1)} %refs_3_.1), custom_call_target="tpu_custom_call" | custom-call | tf_op jit(solution)/shard_map/group_attention/pallas_call | solution.py:326
  57.5 2.3 %copy.7 = bf16[128,4096]{1,0:T(8,128)(2,1)} copy(bf16[128,4096]{1,0:T(8,128)(2,1)} %group_attention.1) | data formatting | bytes 2097152
